TPU v7x, 32 devices: a whole 2x2x4 slice. The times are simulated.
32 devices in a mesh: tm: 8 (over y, x, core), group: 4 (over z).
Axes of the slice: x: 2, y: 2, z: 4, core: 2. Of those that a mesh axis runs over, the one named last changes fastest.
Arguments:
- tokens: bfloat16 [8, 1024, 1024], P('tm', 'group'), may hold values from -6 to 6
- conv_weight: float32 [3, 1024], replicated, may hold values from -3 to 3
- qkv_weight: bfloat16 [1024, 3072], replicated, may hold values from -0.1875 to 0.1875
- attn_out_weight: bfloat16 [1024, 1024], replicated, may hold values from -0.1875 to 0.1875
- router_weight: bfloat16 [1024, 16], replicated, may hold values from -0.375 to 0.375
- expert_ids: int32 [8, 1024, 2], P('tm', 'group'), may hold values from 0 to 15, as said below
- expert_in: bfloat16 [32, 1024, 2048], P(('tm', 'group')), may hold values from -0.1875 to 0.1875
- expert_out: bfloat16 [32, 2048, 1024], P(('tm', 'group')), may hold values from -0.09375 to 0.09375
Outputs:
- layer_out: bfloat16 [8, 1024, 1024], P('tm', 'group')
Inputs may be any that keep to these rules, and one draw needn't show every extreme that they name: `expert_ids`: each row names two different experts. In the rows of one device (one frame, 256 consecutive spatial positions) * 4 experts are named exactly 64 times each and the others share the remaining routes as evenly as possible; one expert is among the fully named ones on every device.
All inputs are finite; a program needn't handle non-finite values.
Results may differ from a plain program's by a relative error of at most 0.0095.
Values may be sent and summed in bfloat16 or wider, within the bound.
No kernel may reach another device: no remote copies, remote signals or barrier semaphores. Data moves between devices by JAX's collectives and lax.ppermute only.
A program may use at most 128 MiB of HBM per device.

v0:
```python
import math
import jax
import jax.numpy as jnp
from jax import lax
from jax.sharding import PartitionSpec as P

HD = 64


def layer_normed(values):
    values = values.astype(jnp.float32)
    centre = jnp.mean(values, -1, keepdims=True)
    spread = jnp.mean((values - centre) ** 2, -1, keepdims=True)
    return ((values - centre) / jnp.sqrt(spread + 1e-05)).astype(jnp.bfloat16)


def unit_scaled(values):
    return (values / jnp.sqrt(jnp.mean(values * values, -1, keepdims=True) + 1e-06)).astype(
        jnp.bfloat16
    )


def convolved(frames, conv_weight):
    wide = frames.astype(jnp.float32)
    padded = jnp.pad(wide, ((1, 1), (0, 0), (0, 0)))
    summed = conv_weight[0] * padded[:-2] + conv_weight[1] * wide + conv_weight[2] * padded[2:]
    return (wide + summed).astype(jnp.bfloat16)


def time_mixing(normed, qkv_weight, attn_out_weight):
    frames, across, channels = normed.shape
    heads = channels // HD
    projected = jnp.dot(
        normed.reshape(frames * across, channels), qkv_weight, preferred_element_type=jnp.float32
    )
    projected = projected.reshape(frames, across, 3, heads, HD)
    queries = unit_scaled(projected[:, :, 0])
    keys_all = unit_scaled(projected[:, :, 1])
    values_all = projected[:, :, 2].astype(jnp.bfloat16)
    scores = jnp.einsum(
        "fshd,gshd->shfg", queries, keys_all, preferred_element_type=jnp.float32
    ) / math.sqrt(HD)
    weights = jnp.exp(scores)
    weights = (weights / jnp.sum(weights, -1, keepdims=True)).astype(jnp.bfloat16)
    context = jnp.einsum(
        "shfg,gshd->fshd", weights, values_all, preferred_element_type=jnp.float32
    ).astype(jnp.bfloat16)
    mixed_out = jnp.dot(
        context.reshape(frames * across, channels),
        attn_out_weight,
        preferred_element_type=jnp.float32,
    )
    return mixed_out.astype(jnp.bfloat16).reshape(frames, across, channels)


def body(
    tokens,
    conv_weight,
    qkv_weight,
    attn_out_weight,
    router_weight,
    expert_ids,
    expert_in,
    expert_out,
):
    shards = lax.axis_size("tm")
    groups = lax.axis_size("group")
    classes = groups // 2
    mine = lax.axis_index("group") // 2
    spatial, channels = tokens.shape[1:]
    across = spatial // shards
    experts = router_weight.shape[1]
    capacity = 4 * spatial // experts

    def swapped(rows, step):
        if step == 0:
            return rows
        return lax.ppermute(rows, "group", [(i, i ^ step) for i in range(groups)])

    routed = expert_ids.reshape(spatial, 2)
    ids = [swapped(routed, step) for step in range(groups)]
    received = lax.all_to_all(
        tokens.reshape(1, shards, across, channels), "tm", split_axis=1, concat_axis=0, tiled=True
    ).reshape(shards, across, channels)
    stream_one = convolved(received, conv_weight)
    attended = time_mixing(layer_normed(stream_one), qkv_weight, attn_out_weight)
    stream_two = (stream_one.astype(jnp.float32) + attended.astype(jnp.float32)).astype(
        jnp.bfloat16
    )
    stream = lax.all_to_all(
        stream_two.reshape(shards, 1, across, channels),
        "tm",
        split_axis=0,
        concat_axis=1,
        tiled=True,
    ).reshape(spatial, channels)
    home = jnp.arange(shards, dtype=jnp.int32) * classes + mine
    blocks = [swapped(stream, step) for step in range(groups)]
    partials = []
    for step in range(groups):
        rows = layer_normed(blocks[step])
        logits = jnp.dot(rows, router_weight, preferred_element_type=jnp.float32)
        matches = ids[step][:, :, None] == jnp.arange(experts, dtype=jnp.int32)
        chosen = jnp.sum(jnp.where(matches, logits[:, None, :], 0.0), -1)
        gates = jax.nn.sigmoid(chosen)
        shares = gates / jnp.sum(gates, -1, keepdims=True)
        here = ids[step][:, :, None] == home
        weight = jnp.sum(jnp.where(here, shares[:, :, None], 0.0), 1)
        member = jnp.any(here, 1)
        order = jnp.arange(spatial, dtype=jnp.int32)
        earlier = (order[:, None] > order[None, :]).astype(jnp.bfloat16)
        rank = jnp.dot(
            earlier, member.astype(jnp.bfloat16), preferred_element_type=jnp.float32
        ).astype(jnp.int32)
        slots = jnp.arange(capacity, dtype=jnp.int32)
        picks = member[:, :, None] & (rank[:, :, None] == slots)
        send = picks.astype(jnp.bfloat16).reshape(spatial, shards * capacity)
        back = jnp.where(picks, weight[:, :, None], 0.0).astype(jnp.bfloat16)
        back = back.reshape(spatial, shards * capacity)
        outbox = lax.dot_general(
            send, rows, (((0,), (0,)), ((), ())), preferred_element_type=jnp.float32
        ).astype(jnp.bfloat16)
        inbox = lax.all_to_all(
            outbox.reshape(shards, capacity, channels),
            "tm",
            split_axis=0,
            concat_axis=0,
            tiled=True,
        ).reshape(shards * capacity, channels)
        hidden = jax.nn.gelu(
            jnp.dot(inbox, expert_in[0], preferred_element_type=jnp.float32)
        ).astype(jnp.bfloat16)
        partial = jnp.dot(hidden, expert_out[0], preferred_element_type=jnp.float32)
        returned = lax.all_to_all(
            partial.astype(jnp.bfloat16).reshape(shards, capacity, channels),
            "tm",
            split_axis=0,
            concat_axis=0,
            tiled=True,
        ).reshape(shards * capacity, channels)
        mixed = jnp.dot(back, returned, preferred_element_type=jnp.float32)
        if step:
            mixed = swapped(mixed.astype(jnp.bfloat16), step).astype(jnp.float32)
        partials.append(mixed)
    total = stream.astype(jnp.float32)
    for mixed in partials:
        total = total + mixed
    return total.astype(jnp.bfloat16).reshape(1, spatial, channels)


def solution(mesh):
    placed = (
        P("tm", "group", None),
        P(),
        P(),
        P(),
        P(),
        P("tm", "group", None),
        P(("tm", "group"), None, None),
        P(("tm", "group"), None, None),
    )
    return jax.shard_map(
        body, mesh=mesh, in_specs=placed, out_specs=P("tm", "group", None), check_vma=False
    )
```

profile of v0, /device:TPU:10, one launch (start us, length us, event | category | flops | bytes accessed | tf_op | source)
XLA Modules:
  0.0 279.0 jit_solution(12095422469277350351)
XLA Ops:
  0.5 2.6 collective-permute-start.3
  3.5 4.3 %all-to-all-start = ((bf16[1,8,32,1024]{3,2,0,1:T(8,128)(2,1)}), bf16[1,8,32,1024]{3,2,0,1:T(8,128)(2,1)S(1)}, u32[]{:S(2)}, u32[]{:S(2)}) async-start(bf16[1,8,32,1024]{3,2,0,1:T(8,128)(2,1)} %bitcast.183), calls=%async_computation | async-start | bytes 1048576 | tf_op jit(solution)/shard_map/all_to_all | solution.py:82
  7.7 0.8 fusion.173
  8.6 8.7 %copy.63 = bf16[1024,3072]{0,1:T(8,128)(2,1)} copy(bf16[1024,3072]{1,0:T(8,128)(2,1)} %param.10) | data formatting | bytes 12582912 | tf_op args[2]
  18.2 0.8 convolution_convert_fusion.6
  18.9 0.8 convolution_convert_fusion.7
  20.5 5.7 %fusion.119 = f32[8,32,3,16,64]{4,1,3,2,0:T(8,128)S(1)} fusion(bf16[3,16,64,1024,1]{3,2,1,0,4:T(8,128)(2,1)} %bitcast.172, bf16[8,32,1024]{2,1,0:T(8,128)(2,1)S(1)} %get-tuple-element.16, f32[8,32]{1,0:T(8,128)S(1)} %add_sqrt_fusion.3, f32[8,32]{1,0:T(8,128)S(1)} %broadcast_multiply_fusion.1), kind=kOutput, calls=%fused_computation.138 | convolution fusion | flops 1611661312 | bytes 9963520 | tf_op jit(solution)/shard_map/dot_general | solution.py:33
  26.2 1.2 multiply_reduce_fusion.1
  27.7 1.4 divide_convert_fusion.2
  29.1 2.8 %fusion.56 = (f32[32,16,8]{2,1,0:T(8,128)S(1)}, f32[32,16,8,8]{2,3,1,0:T(8,128)S(1)}) fusion(bf16[8,32,16,64]{3,1,2,0:T(8,128)(2,1)S(1)} %get-tuple-element.18, bf16[8,32,16,64]{3,1,2,0:T(8,128)(2,1)S(1)} %get-tuple-element.17), kind=kOutput, calls=%fused_computation.61 | convolution fusion | flops 4255744 | bytes 1196032 | tf_op jit(solution)/shard_map/fshd,gshd->shfg/dot_general | solution.py:40
  32.0 1.5 fusion.69
  33.5 1.2 copy.68
  34.6 1.9 reshape.364
  36.6 0.7 convolution_convert_fusion.5
  37.3 1.0 fusion.117
  38.3 4.2 %all-to-all-start.1 = ((bf16[8,1,32,1024]{3,2,1,0:T(8,128)(2,1)}), bf16[8,1,32,1024]{3,2,1,0:T(8,128)(2,1)S(1)}, u32[]{:S(2)}, u32[]{:S(2)}) async-start(bf16[8,1,32,1024]{3,2,1,0:T(8,128)(2,1)} %fusion.117), calls=%async_computation.1 | async-start | bytes 1048576 | tf_op jit(solution)/shard_map/all_to_all | solution.py:90
  42.7 1.1 fusion.129
  44.6 0.7 fusion.125
  45.3 5.5 %all-to-all-done.1 = bf16[8,1,32,1024]{3,2,1,0:T(8,128)(2,1)S(1)} async-done(((bf16[8,1,32,1024]{3,2,1,0:T(8,128)(2,1)}), bf16[8,1,32,1024]{3,2,1,0:T(8,128)(2,1)S(1)}, u32[]{:S(2)}, u32[]{:S(2)}) %all-to-all-start.1) | async-done | bytes 524320 | tf_op jit(solution)/shard_map/all_to_all | solution.py:90
  50.8 1.3 collective-permute-start.1
  52.1 2.1 collective-permute-start.4
  56.8 2.4 convolution_convert_fusion.3
  59.2 5.6 %all-to-all-start.2 = ((bf16[8,64,1024]{2,1,0:T(8,128)(2,1)}), bf16[8,64,1024]{2,1,0:T(8,128)(2,1)}, u32[]{:S(2)}, u32[]{:S(2)}) async-start(bf16[8,64,1024]{2,1,0:T(8,128)(2,1)} %bitcast.173), calls=%async_computation.2 | async-start | bytes 2097152 | tf_op jit(solution)/shard_map/all_to_all | solution.py:123
  64.7 1.2 fusion.123
  66.6 7.6 %collective-permute-done.1 = bf16[256,1024]{1,0:T(8,128)(2,1)} collective-permute-done((bf16[256,1024]{1,0:T(8,128)(2,1)S(1)}, bf16[256,1024]{1,0:T(8,128)(2,1)}, u32[]{:S(2)}, u32[]{:S(2)}) %collective-permute-start.1) | collective-permute-done | bytes 524320 | tf_op jit(solution)/shard_map/ppermute | solution.py:78
  74.2 1.2 convert_reduce_fusion.3
  75.4 1.3 fusion.89
  76.7 1.3 fusion.90
  78.2 10.9 %collective-permute-done.4 = bf16[256,1024]{1,0:T(8,128)(2,1)} collective-permute-done((bf16[256,1024]{1,0:T(8,128)(2,1)S(1)}, bf16[256,1024]{1,0:T(8,128)(2,1)}, u32[]{:S(2)}, u32[]{:S(2)}) %collective-permute-start.4) | collective-permute-done | bytes 524320 | tf_op jit(solution)/shard_map/ppermute | solution.py:78
  89.1 1.2 convert_reduce_fusion.2
  90.3 1.3 fusion.87
  91.6 1.3 fusion.88
  93.1 7.3 %collective-permute-done.7 = bf16[256,1024]{1,0:T(8,128)(2,1)S(1)} collective-permute-done((bf16[256,1024]{1,0:T(8,128)(2,1)S(1)}, bf16[256,1024]{1,0:T(8,128)(2,1)S(1)}, u32[]{:S(2)}, u32[]{:S(2)}) %collective-permute-start.7) | collective-permute-done | bytes 524320 | tf_op jit(solution)/shard_map/ppermute | solution.py:78
  102.1 1.0 fusion.86
  103.1 1.4 convolution_convert_fusion.2
  104.6 4.2 %all-to-all-start.4 = ((bf16[8,64,1024]{2,1,0:T(8,128)(2,1)}), bf16[8,64,1024]{2,1,0:T(8,128)(2,1)}, u32[]{:S(2)}, u32[]{:S(2)}) async-start(bf16[8,64,1024]{2,1,0:T(8,128)(2,1)} %bitcast.175), calls=%async_computation.4 | async-start | bytes 2097152 | tf_op jit(solution)/shard_map/all_to_all | solution.py:123
  109.5 1.3 fusion.176
  111.5 2.5 convolution_convert_fusion.1
  113.9 7.9 %all-to-all-done.4 = bf16[8,64,1024]{2,1,0:T(8,128)(2,1)} async-done(((bf16[8,64,1024]{2,1,0:T(8,128)(2,1)}), bf16[8,64,1024]{2,1,0:T(8,128)(2,1)}, u32[]{:S(2)}, u32[]{:S(2)}) %all-to-all-start.4) | async-done | bytes 1048608 | tf_op jit(solution)/shard_map/all_to_all | solution.py:123
  121.9 5.6 %all-to-all-start.6 = ((bf16[8,64,1024]{2,1,0:T(8,128)(2,1)}), bf16[8,64,1024]{2,1,0:T(8,128)(2,1)}, u32[]{:S(2)}, u32[]{:S(2)}) async-start(bf16[8,64,1024]{2,1,0:T(8,128)(2,1)} %bitcast.174), calls=%async_computation.6 | async-start | bytes 2097152 | tf_op jit(solution)/shard_map/all_to_all | solution.py:123
  128.2 0.8 fusion.146
  129.0 1.4 convolution_convert_fusion
  130.4 11.1 %all-to-all-done.6 = bf16[8,64,1024]{2,1,0:T(8,128)(2,1)} async-done(((bf16[8,64,1024]{2,1,0:T(8,128)(2,1)}), bf16[8,64,1024]{2,1,0:T(8,128)(2,1)}, u32[]{:S(2)}, u32[]{:S(2)}) %all-to-all-start.6) | async-done | bytes 1048608 | tf_op jit(solution)/shard_map/all_to_all | solution.py:123
  141.5 5.6 %all-to-all-start.8 = ((bf16[8,64,1024]{2,1,0:T(8,128)(2,1)}), bf16[8,64,1024]{2,1,0:T(8,128)(2,1)}, u32[]{:S(2)}, u32[]{:S(2)}) async-start(bf16[8,64,1024]{2,1,0:T(8,128)(2,1)} %bitcast.176), calls=%async_computation.8 | async-start | bytes 2097152 | tf_op jit(solution)/shard_map/all_to_all | solution.py:123
  147.1 9.3 %fusion.60 = bf16[512,1024]{1,0:T(8,128)(2,1)} fusion(bf16[1,2048,1024]{2,1,0:T(8,128)(2,1)} %param.15, bf16[512,1024]{1,0:T(8,128)(2,1)} %bitcast.31, bf16[1,1024,2048]{2,1,0:T(8,128)(2,1)} %param.14), kind=kOutput, calls=%fused_computation.71 | convolution fusion | flops 4304928768 | bytes 10485760 | tf_op jit(solution)/shard_map/dot_general | solution.py:133
  156.5 4.6 %all-to-all-done.8 = bf16[8,64,1024]{2,1,0:T(8,128)(2,1)} async-done(((bf16[8,64,1024]{2,1,0:T(8,128)(2,1)}), bf16[8,64,1024]{2,1,0:T(8,128)(2,1)}, u32[]{:S(2)}, u32[]{:S(2)}) %all-to-all-start.8) | async-done | bytes 1048608 | tf_op jit(solution)/shard_map/all_to_all | solution.py:123
  161.1 5.6 %all-to-all-start.5 = ((bf16[8,64,1024]{2,1,0:T(8,128)(2,1)}), bf16[8,64,1024]{2,1,0:T(8,128)(2,1)}, u32[]{:S(2)}, u32[]{:S(2)}) async-start(bf16[8,64,1024]{2,1,0:T(8,128)(2,1)} %bitcast.180), calls=%async_computation.5 | async-start | bytes 2097152 | tf_op jit(solution)/shard_map/all_to_all | solution.py:134
  166.8 9.4 %fusion.63 = bf16[512,1024]{1,0:T(8,128)(2,1)} fusion(bf16[1,2048,1024]{2,1,0:T(8,128)(2,1)} %param.15, bf16[512,1024]{1,0:T(8,128)(2,1)} %bitcast.37, bf16[1,1024,2048]{2,1,0:T(8,128)(2,1)} %param.14), kind=kOutput, calls=%fused_computation.72 | convolution fusion | flops 4304928768 | bytes 10485760 | tf_op jit(solution)/shard_map/dot_general | solution.py:133
  176.1 4.6 %all-to-all-done.5 = bf16[8,64,1024]{2,1,0:T(8,128)(2,1)} async-done(((bf16[8,64,1024]{2,1,0:T(8,128)(2,1)}), bf16[8,64,1024]{2,1,0:T(8,128)(2,1)}, u32[]{:S(2)}, u32[]{:S(2)}) %all-to-all-start.5) | async-done | bytes 1048608 | tf_op jit(solution)/shard_map/all_to_all | solution.py:134
  180.8 5.6 %all-to-all-start.7 = ((bf16[8,64,1024]{2,1,0:T(8,128)(2,1)}), bf16[8,64,1024]{2,1,0:T(8,128)(2,1)}, u32[]{:S(2)}, u32[]{:S(2)}) async-start(bf16[8,64,1024]{2,1,0:T(8,128)(2,1)} %bitcast.181), calls=%async_computation.7 | async-start | bytes 2097152 | tf_op jit(solution)/shard_map/all_to_all | solution.py:134
  186.4 9.4 %fusion.66 = bf16[512,1024]{1,0:T(8,128)(2,1)} fusion(bf16[1,2048,1024]{2,1,0:T(8,128)(2,1)} %param.15, bf16[512,1024]{1,0:T(8,128)(2,1)} %bitcast.43, bf16[1,1024,2048]{2,1,0:T(8,128)(2,1)} %param.14), kind=kOutput, calls=%fused_computation.73 | convolution fusion | flops 4304928768 | bytes 10485760 | tf_op jit(solution)/shard_map/dot_general | solution.py:133
  195.8 4.6 %all-to-all-done.7 = bf16[8,64,1024]{2,1,0:T(8,128)(2,1)} async-done(((bf16[8,64,1024]{2,1,0:T(8,128)(2,1)}), bf16[8,64,1024]{2,1,0:T(8,128)(2,1)}, u32[]{:S(2)}, u32[]{:S(2)}) %all-to-all-start.7) | async-done | bytes 1048608 | tf_op jit(solution)/shard_map/all_to_all | solution.py:134
  200.4 5.6 %all-to-all-start.9 = ((bf16[8,64,1024]{2,1,0:T(8,128)(2,1)}), bf16[8,64,1024]{2,1,0:T(8,128)(2,1)}, u32[]{:S(2)}, u32[]{:S(2)}) async-start(bf16[8,64,1024]{2,1,0:T(8,128)(2,1)} %bitcast.179), calls=%async_computation.9 | async-start | bytes 2097152 | tf_op jit(solution)/shard_map/all_to_all | solution.py:134
  206.0 9.4 %fusion.57 = bf16[512,1024]{1,0:T(8,128)(2,1)} fusion(bf16[1,2048,1024]{2,1,0:T(8,128)(2,1)} %param.15, bf16[512,1024]{1,0:T(8,128)(2,1)} %bitcast.23, bf16[1,1024,2048]{2,1,0:T(8,128)(2,1)} %param.14), kind=kOutput, calls=%fused_computation.70 | convolution fusion | flops 4304928768 | bytes 10485760 | tf_op jit(solution)/shard_map/dot_general | solution.py:133
  215.5 2.5 fusion.70
  218.0 2.0 all-to-all-done.9
  220.0 5.8 %all-to-all-start.3 = ((bf16[8,64,1024]{2,1,0:T(8,128)(2,1)}), bf16[8,64,1024]{2,1,0:T(8,128)(2,1)}, u32[]{:S(2)}, u32[]{:S(2)}) async-start(bf16[8,64,1024]{2,1,0:T(8,128)(2,1)} %bitcast.178), calls=%async_computation.3 | async-start | bytes 2097152 | tf_op jit(solution)/shard_map/all_to_all | solution.py:134
  225.8 2.5 fusion.71
  228.3 2.5 fusion.72
  230.9 1.5 collective-permute-start.8
  232.3 7.5 %all-to-all-done.3 = bf16[8,64,1024]{2,1,0:T(8,128)(2,1)} async-done(((bf16[8,64,1024]{2,1,0:T(8,128)(2,1)}), bf16[8,64,1024]{2,1,0:T(8,128)(2,1)}, u32[]{:S(2)}, u32[]{:S(2)}) %all-to-all-start.3) | async-done | bytes 1048608 | tf_op jit(solution)/shard_map/all_to_all | solution.py:134
  239.8 23.7 %collective-permute-done.5 = bf16[256,1024]{1,0:T(8,128)(2,1)} collective-permute-done((bf16[256,1024]{1,0:T(8,128)(2,1)}, bf16[256,1024]{1,0:T(8,128)(2,1)}, u32[]{:S(2)}, u32[]{:S(2)}) %collective-permute-start.5) | collective-permute-done | bytes 524320 | tf_op jit(solution)/shard_map/ppermute | solution.py:78
  263.5 12.5 %collective-permute-done.8 = bf16[256,1024]{1,0:T(8,128)(2,1)} collective-permute-done((bf16[256,1024]{1,0:T(8,128)(2,1)}, bf16[256,1024]{1,0:T(8,128)(2,1)}, u32[]{:S(2)}, u32[]{:S(2)}) %collective-permute-start.8) | collective-permute-done | bytes 524320 | tf_op jit(solution)/shard_map/ppermute | solution.py:78
  276.0 3.0 %fusion.116 = bf16[1,256,1024]{2,1,0:T(8,128)(2,1)} fusion(bf16[256,1024]{1,0:T(8,128)(2,1)} %collective-permute-done.8, bf16[256,1024]{1,0:T(8,128)(2,1)} %collective-permute-done.5, bf16[256,1024]{1,0:T(8,128)(2,1)S(1)} %collective-permute-done.2, bf16[8,64,1024]{2,1,0:T(8,128)(2,1)} %all-to-all-done.3, bf16[256,1024]{1,0:T(8,128)(2,1)S(1)} %bitcast.171, ...), kind=kOutput, calls=%fused_computation.135 | convolution fusion | flops 271187968 | bytes 3684352 | tf_op jit(solution)/shard_map/dot_general | solution.py:141
  (103 shorter events, 11.2 us)
Async XLA Ops:
  0.0 36.6 %copy-start = (bf16[1024,1024]{1,0:T(8,128)(2,1)S(1)}, bf16[1024,1024]{1,0:T(8,128)(2,1)}, u32[]{:S(2)}) copy-start(bf16[1024,1024]{1,0:T(8,128)(2,1)} %param.11) | copy-start | bytes 6291460
  0.0 18.0 %collective-permute-start = (s32[256,2]{0,1:T(2,128)}, s32[256,2]{0,1:T(2,128)S(1)}, u32[]{:S(2)}, u32[]{:S(2)}) collective-permute-start(s32[256,2]{0,1:T(2,128)} %bitcast.185), channel_id=1, source_target_pairs={{0,1},{1,0},{2,3},{3,2},{4,5},{5,4},{6,7},{7,6},{8,9},{9,8},{10,11... | collective-permute-start | bytes 6152 | tf_op jit(solution)/shard_map/ppermute | solution.py:78
  0.5 17.5 %collective-permute-start.3 = (s32[256,2]{0,1:T(2,128)}, s32[256,2]{0,1:T(2,128)S(1)}, u32[]{:S(2)}, u32[]{:S(2)}) collective-permute-start(s32[256,2]{0,1:T(2,128)} %bitcast.186), channel_id=1, source_target_pairs={{0,2},{1,3},{2,0},{3,1},{4,6},{5,7},{6,4},{7,5},{8,10},{9,11},{10,... | collective-permute-start | bytes 6152 | tf_op jit(solution)/shard_map/ppermute | solution.py:78
  3.0 15.0 %collective-permute-start.6 = (s32[256,2]{0,1:T(2,128)}, s32[256,2]{0,1:T(2,128)S(1)}, u32[]{:S(2)}, u32[]{:S(2)}) collective-permute-start(s32[256,2]{0,1:T(2,128)} %bitcast.187), channel_id=1, source_target_pairs={{0,3},{1,2},{2,1},{3,0},{4,7},{5,6},{6,5},{7,4},{8,11},{9,10},{10,... | collective-permute-start | bytes 6152 | tf_op jit(solution)/shard_map/ppermute | solution.py:78
  3.5 16.2 %all-to-all-start = ((bf16[1,8,32,1024]{3,2,0,1:T(8,128)(2,1)}), bf16[1,8,32,1024]{3,2,0,1:T(8,128)(2,1)S(1)}, u32[]{:S(2)}, u32[]{:S(2)}) async-start(bf16[1,8,32,1024]{3,2,0,1:T(8,128)(2,1)} %bitcast.183), calls=%async_computation | async-start | bytes 1048576 | tf_op jit(solution)/shard_map/all_to_all | solution.py:82
  8.6 9.4 %copy-start.24 = (s32[8]{0:T(128)}, s32[8]{0:T(128)S(1)}, u32[]{:S(2)}) copy-start(s32[8]{0:T(128)S(1)} %multiply_add_fusion) | copy-start | bytes 100
  8.6 9.4 %copy-start.4 = (s32[1,256,2]{1,2,0:T(2,128)S(1)}, s32[1,256,2]{1,2,0:T(2,128)}, u32[]{:S(2)}) copy-start(s32[1,256,2]{1,2,0:T(2,128)} %param.13) | copy-start | bytes 6148
  18.0 8.2 %copy-start.5 = (s32[256,2]{0,1:T(2,128)}, s32[256,2]{0,1:T(2,128)S(1)}, u32[]{:S(2)}) copy-start(s32[256,2]{0,1:T(2,128)S(1)} %collective-permute-done.3) | copy-start | bytes 6148
  18.0 8.2 %copy-start.7 = (s32[256,2]{0,1:T(2,128)}, s32[256,2]{0,1:T(2,128)S(1)}, u32[]{:S(2)}) copy-start(s32[256,2]{0,1:T(2,128)S(1)} %collective-permute-done.6) | copy-start | bytes 6148
  18.1 1.7 copy-start.20
  18.1 24.4 %copy-start.22 = (pred[256,8]{0,1:T(8,128)(4,1)}, pred[256,8]{0,1:T(8,128)(4,1)S(1)}, u32[]{:S(2)}) copy-start(pred[256,8]{0,1:T(8,128)(4,1)S(1)} %get-tuple-element.12) | copy-start | bytes 6148
  18.1 24.5 %copy-start.18 = (pred[256,8]{0,1:T(8,128)(4,1)}, pred[256,8]{0,1:T(8,128)(4,1)S(1)}, u32[]{:S(2)}) copy-start(pred[256,8]{0,1:T(8,128)(4,1)S(1)} %get-tuple-element.14) | copy-start | bytes 6148
  18.1 25.8 %copy-start.10 = (pred[256,8]{0,1:T(8,128)(4,1)}, pred[256,8]{0,1:T(8,128)(4,1)S(1)}, u32[]{:S(2)}) copy-start(pred[256,8]{0,1:T(8,128)(4,1)S(1)} %get-tuple-element.11) | copy-start | bytes 6148
  38.3 12.5 %all-to-all-start.1 = ((bf16[8,1,32,1024]{3,2,1,0:T(8,128)(2,1)}), bf16[8,1,32,1024]{3,2,1,0:T(8,128)(2,1)S(1)}, u32[]{:S(2)}, u32[]{:S(2)}) async-start(bf16[8,1,32,1024]{3,2,1,0:T(8,128)(2,1)} %fusion.117), calls=%async_computation.1 | async-start | bytes 1048576 | tf_op jit(solution)/shard_map/all_to_all | solution.py:90
  42.7 1.3 copy-start.16
  43.9 0.6 copy-start.12
  50.8 23.4 %collective-permute-start.1 = (bf16[256,1024]{1,0:T(8,128)(2,1)S(1)}, bf16[256,1024]{1,0:T(8,128)(2,1)}, u32[]{:S(2)}, u32[]{:S(2)}) collective-permute-start(bf16[256,1024]{1,0:T(8,128)(2,1)S(1)} %bitcast.167), channel_id=1, source_target_pairs={{0,1},{1,0},{2,3},{3,2},{4,5},{5,4},{6,7},{7,6},{8,9},{9,8},{10,11... | collective-permute-start | bytes 1572872 | tf_op jit(solution)/shard_map/ppermute | solution.py:78
  52.1 37.0 %collective-permute-start.4 = (bf16[256,1024]{1,0:T(8,128)(2,1)S(1)}, bf16[256,1024]{1,0:T(8,128)(2,1)}, u32[]{:S(2)}, u32[]{:S(2)}) collective-permute-start(bf16[256,1024]{1,0:T(8,128)(2,1)S(1)} %bitcast.168), channel_id=1, source_target_pairs={{0,2},{1,3},{2,0},{3,1},{4,6},{5,7},{6,4},{7,5},{8,10},{9,11},{10,... | collective-permute-start | bytes 1572872 | tf_op jit(solution)/shard_map/ppermute | solution.py:78
  54.3 46.2 %collective-permute-start.7 = (bf16[256,1024]{1,0:T(8,128)(2,1)S(1)}, bf16[256,1024]{1,0:T(8,128)(2,1)S(1)}, u32[]{:S(2)}, u32[]{:S(2)}) collective-permute-start(bf16[256,1024]{1,0:T(8,128)(2,1)S(1)} %bitcast.169), channel_id=1, source_target_pairs={{0,3},{1,2},{2,1},{3,0},{4,7},{5,6},{6,5},{7,4},{8,11},{9,10},{10,... | collective-permute-start | bytes 1572872 | tf_op jit(solution)/shard_map/ppermute | solution.py:78
  59.2 45.4 %all-to-all-start.2 = ((bf16[8,64,1024]{2,1,0:T(8,128)(2,1)}), bf16[8,64,1024]{2,1,0:T(8,128)(2,1)}, u32[]{:S(2)}, u32[]{:S(2)}) async-start(bf16[8,64,1024]{2,1,0:T(8,128)(2,1)} %bitcast.173), calls=%async_computation.2 | async-start | bytes 2097152 | tf_op jit(solution)/shard_map/all_to_all | solution.py:123
  64.7 13.2 %copy-start.3 = (bf16[1024,16]{0,1:T(8,128)(2,1)S(1)}, bf16[1024,16]{0,1:T(8,128)(2,1)}, u32[]{:S(2)}) copy-start(bf16[1024,16]{0,1:T(8,128)(2,1)} %param.12) | copy-start | bytes 98308
  64.7 35.9 %copy-start.6 = (s32[256,2]{0,1:T(2,128)S(1)}, s32[256,2]{0,1:T(2,128)}, u32[]{:S(2)}) copy-start(s32[256,2]{0,1:T(2,128)} %copy-done.5) | copy-start | bytes 6148
  91.6 19.1 %copy-start.8 = (s32[256,2]{0,1:T(2,128)S(1)}, s32[256,2]{0,1:T(2,128)}, u32[]{:S(2)}) copy-start(s32[256,2]{0,1:T(2,128)} %copy-done.7) | copy-start | bytes 6148
  92.9 10.3 %copy-start.2 = (bf16[256,1024]{1,0:T(8,128)(2,1)}, bf16[256,1024]{1,0:T(8,128)(2,1)S(1)}, u32[]{:S(2)}) copy-start(bf16[256,1024]{1,0:T(8,128)(2,1)S(1)} %fusion.88) | copy-start | bytes 1572868
  100.6 2.5 copy-start.9
  103.1 25.8 %copy-start.1 = (bf16[256,1024]{1,0:T(8,128)(2,1)S(1)}, bf16[256,1024]{1,0:T(8,128)(2,1)}, u32[]{:S(2)}) copy-start(bf16[256,1024]{1,0:T(8,128)(2,1)} %fusion.86) | copy-start | bytes 1572868
  104.6 17.3 %all-to-all-start.4 = ((bf16[8,64,1024]{2,1,0:T(8,128)(2,1)}), bf16[8,64,1024]{2,1,0:T(8,128)(2,1)}, u32[]{:S(2)}, u32[]{:S(2)}) async-start(bf16[8,64,1024]{2,1,0:T(8,128)(2,1)} %bitcast.175), calls=%async_computation.4 | async-start | bytes 2097152 | tf_op jit(solution)/shard_map/all_to_all | solution.py:123
  121.9 19.6 %all-to-all-start.6 = ((bf16[8,64,1024]{2,1,0:T(8,128)(2,1)}), bf16[8,64,1024]{2,1,0:T(8,128)(2,1)}, u32[]{:S(2)}, u32[]{:S(2)}) async-start(bf16[8,64,1024]{2,1,0:T(8,128)(2,1)} %bitcast.174), calls=%async_computation.6 | async-start | bytes 2097152 | tf_op jit(solution)/shard_map/all_to_all | solution.py:123
  141.5 19.6 %all-to-all-start.8 = ((bf16[8,64,1024]{2,1,0:T(8,128)(2,1)}), bf16[8,64,1024]{2,1,0:T(8,128)(2,1)}, u32[]{:S(2)}, u32[]{:S(2)}) async-start(bf16[8,64,1024]{2,1,0:T(8,128)(2,1)} %bitcast.176), calls=%async_computation.8 | async-start | bytes 2097152 | tf_op jit(solution)/shard_map/all_to_all | solution.py:123
  161.1 19.6 %all-to-all-start.5 = ((bf16[8,64,1024]{2,1,0:T(8,128)(2,1)}), bf16[8,64,1024]{2,1,0:T(8,128)(2,1)}, u32[]{:S(2)}, u32[]{:S(2)}) async-start(bf16[8,64,1024]{2,1,0:T(8,128)(2,1)} %bitcast.180), calls=%async_computation.5 | async-start | bytes 2097152 | tf_op jit(solution)/shard_map/all_to_all | solution.py:134
  180.8 19.6 %all-to-all-start.7 = ((bf16[8,64,1024]{2,1,0:T(8,128)(2,1)}), bf16[8,64,1024]{2,1,0:T(8,128)(2,1)}, u32[]{:S(2)}, u32[]{:S(2)}) async-start(bf16[8,64,1024]{2,1,0:T(8,128)(2,1)} %bitcast.181), calls=%async_computation.7 | async-start | bytes 2097152 | tf_op jit(solution)/shard_map/all_to_all | solution.py:134
  200.4 19.6 %all-to-all-start.9 = ((bf16[8,64,1024]{2,1,0:T(8,128)(2,1)}), bf16[8,64,1024]{2,1,0:T(8,128)(2,1)}, u32[]{:S(2)}, u32[]{:S(2)}) async-start(bf16[8,64,1024]{2,1,0:T(8,128)(2,1)} %bitcast.179), calls=%async_computation.9 | async-start | bytes 2097152 | tf_op jit(solution)/shard_map/all_to_all | solution.py:134
  206.0 9.4 %copy-start.17 = (s32[256,8]{0,1:T(8,128)S(1)}, s32[256,8]{0,1:T(8,128)}, u32[]{:S(2)}) copy-start(s32[256,8]{0,1:T(8,128)} %copy-done.16) | copy-start | bytes 24580
  206.0 9.4 %copy-start.23 = (pred[256,8]{0,1:T(8,128)(4,1)S(1)}, pred[256,8]{0,1:T(8,128)(4,1)}, u32[]{:S(2)}) copy-start(pred[256,8]{0,1:T(8,128)(4,1)} %copy-done.22) | copy-start | bytes 6148
  215.4 10.4 %copy-start.15 = (s32[256,8]{0,1:T(8,128)S(1)}, s32[256,8]{0,1:T(8,128)}, u32[]{:S(2)}) copy-start(s32[256,8]{0,1:T(8,128)} %convolution_convert_fusion.7) | copy-start | bytes 24580
  215.4 10.4 %copy-start.21 = (pred[256,8]{0,1:T(8,128)(4,1)S(1)}, pred[256,8]{0,1:T(8,128)(4,1)}, u32[]{:S(2)}) copy-start(pred[256,8]{0,1:T(8,128)(4,1)} %copy-done.20) | copy-start | bytes 6148
  215.4 12.9 %copy-start.14 = (s32[256,8]{0,1:T(8,128)S(1)}, s32[256,8]{0,1:T(8,128)}, u32[]{:S(2)}) copy-start(s32[256,8]{0,1:T(8,128)} %convolution_convert_fusion.6) | copy-start | bytes 24580
  215.4 12.9 %copy-start.19 = (pred[256,8]{0,1:T(8,128)(4,1)S(1)}, pred[256,8]{0,1:T(8,128)(4,1)}, u32[]{:S(2)}) copy-start(pred[256,8]{0,1:T(8,128)(4,1)} %copy-done.18) | copy-start | bytes 6148
  218.0 21.8 %collective-permute-start.2 = (bf16[256,1024]{1,0:T(8,128)(2,1)}, bf16[256,1024]{1,0:T(8,128)(2,1)S(1)}, u32[]{:S(2)}, u32[]{:S(2)}) collective-permute-start(bf16[256,1024]{1,0:T(8,128)(2,1)} %fusion.70), channel_id=1, source_target_pairs={{0,1},{1,0},{2,3},{3,2},{4,5},{5,4},{6,7},{7,6},{8,9},{9,8},{10,11... | collective-permute-start | bytes 1572872 | tf_op jit(solution)/shard_map/ppermute | solution.py:78
  220.0 56.0 %copy-start.11 = (pred[256,8]{0,1:T(8,128)(4,1)S(1)}, pred[256,8]{0,1:T(8,128)(4,1)}, u32[]{:S(2)}) copy-start(pred[256,8]{0,1:T(8,128)(4,1)} %copy-done.10) | copy-start | bytes 6148
  220.0 56.0 %copy-start.13 = (s32[256,8]{0,1:T(8,128)S(1)}, s32[256,8]{0,1:T(8,128)}, u32[]{:S(2)}) copy-start(s32[256,8]{0,1:T(8,128)} %copy-done.12) | copy-start | bytes 24580
  220.0 19.8 %all-to-all-start.3 = ((bf16[8,64,1024]{2,1,0:T(8,128)(2,1)}), bf16[8,64,1024]{2,1,0:T(8,128)(2,1)}, u32[]{:S(2)}, u32[]{:S(2)}) async-start(bf16[8,64,1024]{2,1,0:T(8,128)(2,1)} %bitcast.178), calls=%async_computation.3 | async-start | bytes 2097152 | tf_op jit(solution)/shard_map/all_to_all | solution.py:134
  228.3 35.1 %collective-permute-start.5 = (bf16[256,1024]{1,0:T(8,128)(2,1)}, bf16[256,1024]{1,0:T(8,128)(2,1)}, u32[]{:S(2)}, u32[]{:S(2)}) collective-permute-start(bf16[256,1024]{1,0:T(8,128)(2,1)} %fusion.71), channel_id=1, source_target_pairs={{0,2},{1,3},{2,0},{3,1},{4,6},{5,7},{6,4},{7,5},{8,10},{9,11},{10,... | collective-permute-start | bytes 1572872 | tf_op jit(solution)/shard_map/ppermute | solution.py:78
  230.9 45.2 %collective-permute-start.8 = (bf16[256,1024]{1,0:T(8,128)(2,1)}, bf16[256,1024]{1,0:T(8,128)(2,1)}, u32[]{:S(2)}, u32[]{:S(2)}) collective-permute-start(bf16[256,1024]{1,0:T(8,128)(2,1)} %fusion.72), channel_id=1, source_target_pairs={{0,3},{1,2},{2,1},{3,0},{4,7},{5,6},{6,5},{7,4},{8,11},{9,10},{10,... | collective-permute-start | bytes 1572872 | tf_op jit(solution)/shard_map/ppermute | solution.py:78
where the time goes:
time: 281 us; the launch traced here: 279 us
  waiting for transfers between devices  110 us (39%)
  matrix products  71.2 us (25%)
  starting transfers between devices  61.2 us (22%)
  other arithmetic  20.7 us (7%)
  local copies, waits for them, and re-layouts  15.5 us (6%)
    ppermute x9, waiting for transfers between devices, swapped(): return lax.ppermute(rows, 'group', [(i, i ^ step) for i in range(groups)])  62 us
    dot_general x4, matrix products, body(): partial = jnp.dot(hidden, expert_out[0], preferred_element_type=jnp.float32)  37.4 us
    all_to_all x4, waiting for transfers between devices, body(): lax.all_to_all(outbox.reshape(shards, capacity, channels), 'tm', split_ax...  23.6 us
    all_to_all x4, starting transfers between devices, body(): lax.all_to_all(partial.astype(jnp.bfloat16).reshape(shards, capacity, cha...  22.7 us
    all_to_all x4, starting transfers between devices, body(): lax.all_to_all(outbox.reshape(shards, capacity, channels), 'tm', split_ax...  21 us
    all_to_all x4, waiting for transfers between devices, body(): lax.all_to_all(partial.astype(jnp.bfloat16).reshape(shards, capacity, cha...  18.8 us
    dot_general x4, matrix products, body(): mixed = jnp.dot(back, returned, preferred_element_type=jnp.float32)  10.5 us
    unnamed x51, local copies, waits for them, and re-layouts  9.39 us
  transfers between devices with their start and end apart: 19, of which 13 were waited for; matrix products, arithmetic and copies ran while one was open for 31% of the time, Pallas kernels for 0%

commit v1 on v0

--- a/solution.py
+++ b/solution.py
@@ -87,12 +87,18 @@
     stream_two = (stream_one.astype(jnp.float32) + attended.astype(jnp.float32)).astype(
         jnp.bfloat16
     )
-    stream = lax.all_to_all(
-        stream_two.reshape(shards, 1, across, channels),
-        "tm",
-        split_axis=0,
-        concat_axis=1,
-        tiled=True,
+    stream = jnp.concatenate(
+        lax.all_to_all(
+            jnp.stack(
+                jnp.split(
+                    stream_two.reshape(shards, 1, across, channels), lax.axis_size("tm"), axis=0
+                )
+            ),
+            "tm",
+            0,
+            0,
+        ),
+        axis=1,
     ).reshape(spatial, channels)
     home = jnp.arange(shards, dtype=jnp.int32) * classes + mine
     blocks = [swapped(stream, step) for step in range(groups)]

time: 281 us -> 278 us (0.989)
  waiting for transfers between devices: 110 us -> 126 us
  other arithmetic: 20.7 us -> 7.18 us
  matrix products: 71.2 us -> 64.8 us
  local copies, waits for them, and re-layouts: 15.5 us -> 20.2 us
  starting transfers between devices: 61.2 us -> 57.8 us
    ppermute x9, waiting for transfers between devices: 62 us -> 70.5 us  [swapped(): return lax.ppermute(rows, 'group', [(i, i ^ step) for i in range(groups)])]
    unnamed x51 -> x22, local copies, waits for them, and re-layouts: 9.39 us -> 15.1 us
    all_to_all x4, waiting for transfers between devices: 23.6 us -> 28.2 us  [body(): lax.all_to_all(outbox.reshape(shards, capacity, channels), 'tm', split_ax...]
    convert_element_type x4, other arithmetic: 3.74 us -> 0.89 us  [layer_normed(): return ((values - centre) / jnp.sqrt(spread + 1e-05)).astype(jnp.bfloat16)]
  transfers between devices with their start and end apart: 19 -> 19, of which waited for: 13 -> 13; matrix products, arithmetic and copies ran while one was open for 31% -> 23% of each run, Pallas kernels for 0% -> 0%
where the time goes in v1:
time: 278 us; the launch traced here: 277 us
  waiting for transfers between devices  126 us (45%)
  matrix products  64.8 us (23%)
  starting transfers between devices  57.8 us (21%)
  local copies, waits for them, and re-layouts  20.2 us (7%)
  other arithmetic  7.18 us (3%)
    ppermute x9, waiting for transfers between devices, swapped(): return lax.ppermute(rows, 'group', [(i, i ^ step) for i in range(groups)])  70.5 us
    dot_general x4, matrix products, body(): partial = jnp.dot(hidden, expert_out[0], preferred_element_type=jnp.float32)  37 us
    all_to_all x4, waiting for transfers between devices, body(): lax.all_to_all(outbox.reshape(shards, capacity, channels), 'tm', split_ax...  28.2 us
    all_to_all x4, starting transfers between devices, body(): lax.all_to_all(partial.astype(jnp.bfloat16).reshape(shards, capacity, cha...  20.6 us
    all_to_all x4, waiting for transfers between devices, body(): lax.all_to_all(partial.astype(jnp.bfloat16).reshape(shards, capacity, cha...  20 us
    all_to_all x4, starting transfers between devices, body(): lax.all_to_all(outbox.reshape(shards, capacity, channels), 'tm', split_ax...  19.7 us
    unnamed x22, local copies, waits for them, and re-layouts  15.1 us
    dot_general x4, matrix products, body(): mixed = jnp.dot(back, returned, preferred_element_type=jnp.float32)  9.61 us
  transfers between devices with their start and end apart: 19, of which 13 were waited for; matrix products, arithmetic and copies ran while one was open for 23% of the time, Pallas kernels for 0%

profile of v1, /device:TPU:10, one launch (start us, length us, event | category | flops | bytes accessed | tf_op | source)
XLA Modules:
  0.0 276.5 jit_solution(2444450063446270409)
XLA Ops:
  0.0 0.4 collective-permute-start
  0.5 2.6 collective-permute-start.3
  3.0 0.5 collective-permute-start.6
  3.5 4.3 %all-to-all-start = ((bf16[1,8,32,1024]{3,2,0,1:T(8,128)(2,1)}), bf16[1,8,32,1024]{3,2,0,1:T(8,128)(2,1)S(1)}, u32[]{:S(2)}, u32[]{:S(2)}) async-start(bf16[1,8,32,1024]{3,2,0,1:T(8,128)(2,1)} %bitcast.212), calls=%async_computation | async-start | bytes 1048576 | tf_op jit(solution)/shard_map/all_to_all | solution.py:82
  7.7 0.8 fusion.180
  8.6 8.7 %copy.62 = bf16[1024,3072]{0,1:T(8,128)(2,1)} copy(bf16[1024,3072]{1,0:T(8,128)(2,1)} %param.10) | data formatting | bytes 12582912 | tf_op args[2]
  18.0 0.4 convert_reduce_fusion
  18.7 5.7 %fusion.118 = f32[8,32,3,16,64]{4,1,3,2,0:T(8,128)S(1)} fusion(bf16[3,16,64,1024,1]{3,2,1,0,4:T(8,128)(2,1)} %bitcast.200, bf16[8,32,1024]{2,1,0:T(8,128)(2,1)S(1)} %get-tuple-element.16, f32[8,32]{1,0:T(8,128)S(1)} %add_sqrt_fusion.3, f32[8,32]{1,0:T(8,128)S(1)} %broadcast_multiply_fusion.1), kind=kOutput, calls=%fused_computation.137 | convolution fusion | flops 1611661312 | bytes 9963520 | tf_op jit(solution)/shard_map/dot_general | solution.py:33
  24.4 1.2 multiply_reduce_fusion.1
  25.8 1.4 divide_convert_fusion.2
  27.2 2.8 %fusion.56 = (f32[32,16,8]{2,1,0:T(8,128)S(1)}, f32[32,16,8,8]{2,3,1,0:T(8,128)S(1)}) fusion(bf16[8,32,16,64]{3,1,2,0:T(8,128)(2,1)S(1)} %get-tuple-element.18, bf16[8,32,16,64]{3,1,2,0:T(8,128)(2,1)S(1)} %get-tuple-element.17), kind=kOutput, calls=%fused_computation.61 | convolution fusion | flops 4255744 | bytes 1196032 | tf_op jit(solution)/shard_map/fshd,gshd->shfg/dot_general | solution.py:40
  30.1 1.5 fusion.69
  31.6 1.2 copy.67
  32.8 1.9 reshape.371
  34.7 0.7 convolution_convert_fusion.5
  35.6 0.6 fusion.152
  36.3 0.6 fusion.151
  36.9 0.6 fusion.150
  37.5 0.6 fusion.149
  38.2 0.6 fusion.148
  38.8 0.6 fusion.147
  39.4 0.6 fusion.146
  40.1 0.6 fusion.145
  40.7 4.2 %all-to-all-start.1 = ((bf16[8,1,1,32,1024]{4,3,2,1,0:T(8,128)(2,1)}), bf16[8,1,1,32,1024]{4,3,2,1,0:T(8,128)(2,1)S(1)}, u32[]{:S(2)}, u32[]{:S(2)}) async-start(bf16[8,1,1,32,1024]{4,3,2,1,0:T(8,128)(2,1)} %fusion.145), calls=%async_computation.1 | async-start | bytes 1048576 | tf_op jit(solution)/shard_map/all_to_all | solution.py:91
  45.1 0.4 fusion.128
  45.7 7.4 %all-to-all-done.1 = bf16[8,1,1,32,1024]{4,3,2,1,0:T(8,128)(2,1)S(1)} async-done(((bf16[8,1,1,32,1024]{4,3,2,1,0:T(8,128)(2,1)}), bf16[8,1,1,32,1024]{4,3,2,1,0:T(8,128)(2,1)S(1)}, u32[]{:S(2)}, u32[]{:S(2)}) %all-to-all-start.1) | async-done | bytes 524320 | tf_op jit(solution)/shard_map/all_to_all | solution.py:91
  53.2 1.3 collective-permute-start.1
  54.5 2.1 collective-permute-start.4
  56.7 0.6 collective-permute-start.7
  58.1 1.5 convolution_convert_fusion.3
  59.5 5.6 %all-to-all-start.2 = ((bf16[8,64,1024]{2,1,0:T(8,128)(2,1)}), bf16[8,64,1024]{2,1,0:T(8,128)(2,1)}, u32[]{:S(2)}, u32[]{:S(2)}) async-start(bf16[8,64,1024]{2,1,0:T(8,128)(2,1)} %bitcast.201), calls=%async_computation.2 | async-start | bytes 2097152 | tf_op jit(solution)/shard_map/all_to_all | solution.py:129
  65.5 11.1 %collective-permute-done.1 = bf16[256,1024]{1,0:T(8,128)(2,1)S(1)} collective-permute-done((bf16[256,1024]{1,0:T(8,128)(2,1)S(1)}, bf16[256,1024]{1,0:T(8,128)(2,1)S(1)}, u32[]{:S(2)}, u32[]{:S(2)}) %collective-permute-start.1) | collective-permute-done | bytes 524320 | tf_op jit(solution)/shard_map/ppermute | solution.py:78
  77.5 14.0 %collective-permute-done.4 = bf16[256,1024]{1,0:T(8,128)(2,1)S(1)} collective-permute-done((bf16[256,1024]{1,0:T(8,128)(2,1)S(1)}, bf16[256,1024]{1,0:T(8,128)(2,1)S(1)}, u32[]{:S(2)}, u32[]{:S(2)}) %collective-permute-start.4) | collective-permute-done | bytes 524320 | tf_op jit(solution)/shard_map/ppermute | solution.py:78
  92.4 10.4 %collective-permute-done.7 = bf16[256,1024]{1,0:T(8,128)(2,1)S(1)} collective-permute-done((bf16[256,1024]{1,0:T(8,128)(2,1)S(1)}, bf16[256,1024]{1,0:T(8,128)(2,1)S(1)}, u32[]{:S(2)}, u32[]{:S(2)}) %collective-permute-start.7) | collective-permute-done | bytes 524320 | tf_op jit(solution)/shard_map/ppermute | solution.py:78
  103.6 1.4 convolution_convert_fusion.2
  105.0 4.2 %all-to-all-start.4 = ((bf16[8,64,1024]{2,1,0:T(8,128)(2,1)}), bf16[8,64,1024]{2,1,0:T(8,128)(2,1)}, u32[]{:S(2)}, u32[]{:S(2)}) async-start(bf16[8,64,1024]{2,1,0:T(8,128)(2,1)} %bitcast.203), calls=%async_computation.4 | async-start | bytes 2097152 | tf_op jit(solution)/shard_map/all_to_all | solution.py:129
  109.5 1.4 convolution_convert_fusion.1
  111.0 11.3 %all-to-all-done.4 = bf16[8,64,1024]{2,1,0:T(8,128)(2,1)} async-done(((bf16[8,64,1024]{2,1,0:T(8,128)(2,1)}), bf16[8,64,1024]{2,1,0:T(8,128)(2,1)}, u32[]{:S(2)}, u32[]{:S(2)}) %all-to-all-start.4) | async-done | bytes 1048608 | tf_op jit(solution)/shard_map/all_to_all | solution.py:129
  122.3 5.0 %all-to-all-start.6 = ((bf16[8,64,1024]{2,1,0:T(8,128)(2,1)}), bf16[8,64,1024]{2,1,0:T(8,128)(2,1)S(1)}, u32[]{:S(2)}, u32[]{:S(2)}) async-start(bf16[8,64,1024]{2,1,0:T(8,128)(2,1)} %bitcast.202), calls=%async_computation.6 | async-start | bytes 2097152 | tf_op jit(solution)/shard_map/all_to_all | solution.py:129
  127.4 1.4 convolution_convert_fusion
  128.8 12.3 %all-to-all-done.6 = bf16[8,64,1024]{2,1,0:T(8,128)(2,1)S(1)} async-done(((bf16[8,64,1024]{2,1,0:T(8,128)(2,1)}), bf16[8,64,1024]{2,1,0:T(8,128)(2,1)S(1)}, u32[]{:S(2)}, u32[]{:S(2)}) %all-to-all-start.6) | async-done | bytes 1048608 | tf_op jit(solution)/shard_map/all_to_all | solution.py:129
  141.2 5.0 %all-to-all-start.8 = ((bf16[8,64,1024]{2,1,0:T(8,128)(2,1)}), bf16[8,64,1024]{2,1,0:T(8,128)(2,1)S(1)}, u32[]{:S(2)}, u32[]{:S(2)}) async-start(bf16[8,64,1024]{2,1,0:T(8,128)(2,1)} %bitcast.48), calls=%async_computation.8 | async-start | bytes 2097152 | tf_op jit(solution)/shard_map/all_to_all | solution.py:129
  146.2 9.3 %fusion.60 = bf16[512,1024]{1,0:T(8,128)(2,1)} fusion(bf16[1,2048,1024]{2,1,0:T(8,128)(2,1)} %param.15, bf16[512,1024]{1,0:T(8,128)(2,1)} %bitcast.37, bf16[1,1024,2048]{2,1,0:T(8,128)(2,1)} %param.14), kind=kOutput, calls=%fused_computation.71 | convolution fusion | flops 4304928768 | bytes 10485760 | tf_op jit(solution)/shard_map/dot_general | solution.py:139
  155.5 4.6 %all-to-all-done.8 = bf16[8,64,1024]{2,1,0:T(8,128)(2,1)S(1)} async-done(((bf16[8,64,1024]{2,1,0:T(8,128)(2,1)}), bf16[8,64,1024]{2,1,0:T(8,128)(2,1)S(1)}, u32[]{:S(2)}, u32[]{:S(2)}) %all-to-all-start.8) | async-done | bytes 1048608 | tf_op jit(solution)/shard_map/all_to_all | solution.py:129
  160.0 1.0 copy-done.4
  161.1 5.0 %all-to-all-start.5 = ((bf16[8,64,1024]{2,1,0:T(8,128)(2,1)}), bf16[8,64,1024]{2,1,0:T(8,128)(2,1)S(1)}, u32[]{:S(2)}, u32[]{:S(2)}) async-start(bf16[8,64,1024]{2,1,0:T(8,128)(2,1)} %bitcast.209), calls=%async_computation.5 | async-start | bytes 2097152 | tf_op jit(solution)/shard_map/all_to_all | solution.py:140
  166.1 9.0 %fusion.63 = bf16[512,1024]{1,0:T(8,128)(2,1)} fusion(bf16[1,2048,1024]{2,1,0:T(8,128)(2,1)} %param.15, bf16[512,1024]{1,0:T(8,128)(2,1)S(1)} %bitcast.205, bf16[1,1024,2048]{2,1,0:T(8,128)(2,1)} %param.14), kind=kOutput, calls=%fused_computation.72 | convolution fusion | flops 4304928768 | bytes 10485760 | tf_op jit(solution)/shard_map/dot_general | solution.py:139
  175.1 4.9 %all-to-all-done.5 = bf16[8,64,1024]{2,1,0:T(8,128)(2,1)S(1)} async-done(((bf16[8,64,1024]{2,1,0:T(8,128)(2,1)}), bf16[8,64,1024]{2,1,0:T(8,128)(2,1)S(1)}, u32[]{:S(2)}, u32[]{:S(2)}) %all-to-all-start.5) | async-done | bytes 1048608 | tf_op jit(solution)/shard_map/all_to_all | solution.py:140
  180.0 1.0 copy-done.3
  180.9 5.0 %all-to-all-start.7 = ((bf16[8,64,1024]{2,1,0:T(8,128)(2,1)}), bf16[8,64,1024]{2,1,0:T(8,128)(2,1)S(1)}, u32[]{:S(2)}, u32[]{:S(2)}) async-start(bf16[8,64,1024]{2,1,0:T(8,128)(2,1)} %bitcast.210), calls=%async_computation.7 | async-start | bytes 2097152 | tf_op jit(solution)/shard_map/all_to_all | solution.py:140
  185.9 9.3 %fusion.66 = bf16[512,1024]{1,0:T(8,128)(2,1)} fusion(bf16[1,2048,1024]{2,1,0:T(8,128)(2,1)} %param.15, bf16[512,1024]{1,0:T(8,128)(2,1)} %bitcast.207, bf16[1,1024,2048]{2,1,0:T(8,128)(2,1)} %param.14), kind=kOutput, calls=%fused_computation.73 | convolution fusion | flops 4304928768 | bytes 10485760 | tf_op jit(solution)/shard_map/dot_general | solution.py:139
  195.2 4.6 %all-to-all-done.7 = bf16[8,64,1024]{2,1,0:T(8,128)(2,1)S(1)} async-done(((bf16[8,64,1024]{2,1,0:T(8,128)(2,1)}), bf16[8,64,1024]{2,1,0:T(8,128)(2,1)S(1)}, u32[]{:S(2)}, u32[]{:S(2)}) %all-to-all-start.7) | async-done | bytes 1048608 | tf_op jit(solution)/shard_map/all_to_all | solution.py:140
  199.8 5.0 %all-to-all-start.9 = ((bf16[8,64,1024]{2,1,0:T(8,128)(2,1)}), bf16[8,64,1024]{2,1,0:T(8,128)(2,1)S(1)}, u32[]{:S(2)}, u32[]{:S(2)}) async-start(bf16[8,64,1024]{2,1,0:T(8,128)(2,1)} %bitcast.208), calls=%async_computation.9 | async-start | bytes 2097152 | tf_op jit(solution)/shard_map/all_to_all | solution.py:140
  204.8 9.4 %fusion.57 = bf16[512,1024]{1,0:T(8,128)(2,1)} fusion(bf16[1,2048,1024]{2,1,0:T(8,128)(2,1)} %param.15, bf16[512,1024]{1,0:T(8,128)(2,1)} %bitcast.29, bf16[1,1024,2048]{2,1,0:T(8,128)(2,1)} %param.14), kind=kOutput, calls=%fused_computation.70 | convolution fusion | flops 4304928768 | bytes 10485760 | tf_op jit(solution)/shard_map/dot_general | solution.py:139
  214.2 2.5 fusion.70
  216.7 2.0 all-to-all-done.9
  218.7 5.6 %all-to-all-start.3 = ((bf16[8,64,1024]{2,1,0:T(8,128)(2,1)}), bf16[8,64,1024]{2,1,0:T(8,128)(2,1)}, u32[]{:S(2)}, u32[]{:S(2)}) async-start(bf16[8,64,1024]{2,1,0:T(8,128)(2,1)} %bitcast.206), calls=%async_computation.3 | async-start | bytes 2097152 | tf_op jit(solution)/shard_map/all_to_all | solution.py:140
  224.3 1.3 fusion.71
  225.7 2.7 fusion.72
  228.3 1.5 collective-permute-start.8
  229.8 8.5 %all-to-all-done.3 = bf16[8,64,1024]{2,1,0:T(8,128)(2,1)} async-done(((bf16[8,64,1024]{2,1,0:T(8,128)(2,1)}), bf16[8,64,1024]{2,1,0:T(8,128)(2,1)}, u32[]{:S(2)}, u32[]{:S(2)}) %all-to-all-start.3) | async-done | bytes 1048608 | tf_op jit(solution)/shard_map/all_to_all | solution.py:140
  238.3 22.5 %collective-permute-done.5 = bf16[256,1024]{1,0:T(8,128)(2,1)} collective-permute-done((bf16[256,1024]{1,0:T(8,128)(2,1)}, bf16[256,1024]{1,0:T(8,128)(2,1)}, u32[]{:S(2)}, u32[]{:S(2)}) %collective-permute-start.5) | collective-permute-done | bytes 524320 | tf_op jit(solution)/shard_map/ppermute | solution.py:78
  260.8 12.6 %collective-permute-done.8 = bf16[256,1024]{1,0:T(8,128)(2,1)} collective-permute-done((bf16[256,1024]{1,0:T(8,128)(2,1)}, bf16[256,1024]{1,0:T(8,128)(2,1)}, u32[]{:S(2)}, u32[]{:S(2)}) %collective-permute-start.8) | collective-permute-done | bytes 524320 | tf_op jit(solution)/shard_map/ppermute | solution.py:78
  273.4 3.1 %fusion.116 = bf16[1,256,1024]{2,1,0:T(8,128)(2,1)} fusion(bf16[256,1024]{1,0:T(8,128)(2,1)} %collective-permute-done.8, bf16[256,1024]{1,0:T(8,128)(2,1)} %collective-permute-done.5, bf16[256,1024]{1,0:T(8,128)(2,1)} %collective-permute-done.2, bf16[8,64,1024]{2,1,0:T(8,128)(2,1)} %all-to-all-done.3, bf16[256,1024]{1,0:T(8,128)(2,1)S(1)} %bitcast.199, ...), kind=kOutput, calls=%fused_computation.135 | convolution fusion | flops 271187968 | bytes 3684352 | tf_op jit(solution)/shard_map/dot_general | solution.py:147
  (75 shorter events, 6.1 us)
Async XLA Ops:
  0.0 34.7 %copy-start = (bf16[1024,1024]{1,0:T(8,128)(2,1)S(1)}, bf16[1024,1024]{1,0:T(8,128)(2,1)}, u32[]{:S(2)}) copy-start(bf16[1024,1024]{1,0:T(8,128)(2,1)} %param.11) | copy-start | bytes 6291460
  0.0 17.4 %collective-permute-start = (s32[256,2]{0,1:T(2,128)}, s32[256,2]{0,1:T(2,128)S(1)}, u32[]{:S(2)}, u32[]{:S(2)}) collective-permute-start(s32[256,2]{0,1:T(2,128)} %bitcast.214), channel_id=1, source_target_pairs={{0,1},{1,0},{2,3},{3,2},{4,5},{5,4},{6,7},{7,6},{8,9},{9,8},{10,11... | collective-permute-start | bytes 6152 | tf_op jit(solution)/shard_map/ppermute | solution.py:78
  0.5 16.9 %collective-permute-start.3 = (s32[256,2]{0,1:T(2,128)}, s32[256,2]{0,1:T(2,128)S(1)}, u32[]{:S(2)}, u32[]{:S(2)}) collective-permute-start(s32[256,2]{0,1:T(2,128)} %bitcast.215), channel_id=1, source_target_pairs={{0,2},{1,3},{2,0},{3,1},{4,6},{5,7},{6,4},{7,5},{8,10},{9,11},{10,... | collective-permute-start | bytes 6152 | tf_op jit(solution)/shard_map/ppermute | solution.py:78
  3.0 14.4 %collective-permute-start.6 = (s32[256,2]{0,1:T(2,128)}, s32[256,2]{0,1:T(2,128)S(1)}, u32[]{:S(2)}, u32[]{:S(2)}) collective-permute-start(s32[256,2]{0,1:T(2,128)} %bitcast.216), channel_id=1, source_target_pairs={{0,3},{1,2},{2,1},{3,0},{4,7},{5,6},{6,5},{7,4},{8,11},{9,10},{10,... | collective-permute-start | bytes 6152 | tf_op jit(solution)/shard_map/ppermute | solution.py:78
  3.5 14.3 %all-to-all-start = ((bf16[1,8,32,1024]{3,2,0,1:T(8,128)(2,1)}), bf16[1,8,32,1024]{3,2,0,1:T(8,128)(2,1)S(1)}, u32[]{:S(2)}, u32[]{:S(2)}) async-start(bf16[1,8,32,1024]{3,2,0,1:T(8,128)(2,1)} %bitcast.212), calls=%async_computation | async-start | bytes 1048576 | tf_op jit(solution)/shard_map/all_to_all | solution.py:82
  8.6 8.8 %copy-start.6 = (s32[1,256,2]{1,2,0:T(2,128)S(1)}, s32[1,256,2]{1,2,0:T(2,128)}, u32[]{:S(2)}) copy-start(s32[1,256,2]{1,2,0:T(2,128)} %param.13) | copy-start | bytes 6148
  37.5 27.6 %copy-start.5 = (bf16[1024,16]{0,1:T(8,128)(2,1)S(1)}, bf16[1024,16]{0,1:T(8,128)(2,1)}, u32[]{:S(2)}) copy-start(bf16[1024,16]{0,1:T(8,128)(2,1)} %param.12) | copy-start | bytes 98308
  40.7 12.5 %all-to-all-start.1 = ((bf16[8,1,1,32,1024]{4,3,2,1,0:T(8,128)(2,1)}), bf16[8,1,1,32,1024]{4,3,2,1,0:T(8,128)(2,1)S(1)}, u32[]{:S(2)}, u32[]{:S(2)}) async-start(bf16[8,1,1,32,1024]{4,3,2,1,0:T(8,128)(2,1)} %fusion.145), calls=%async_computation.1 | async-start | bytes 1048576 | tf_op jit(solution)/shard_map/all_to_all | solution.py:91
  53.2 23.4 %collective-permute-start.1 = (bf16[256,1024]{1,0:T(8,128)(2,1)S(1)}, bf16[256,1024]{1,0:T(8,128)(2,1)S(1)}, u32[]{:S(2)}, u32[]{:S(2)}) collective-permute-start(bf16[256,1024]{1,0:T(8,128)(2,1)S(1)} %bitcast.195), channel_id=1, source_target_pairs={{0,1},{1,0},{2,3},{3,2},{4,5},{5,4},{6,7},{7,6},{8,9},{9,8},{10,11... | collective-permute-start | bytes 1572872 | tf_op jit(solution)/shard_map/ppermute | solution.py:78
  54.5 37.0 %collective-permute-start.4 = (bf16[256,1024]{1,0:T(8,128)(2,1)S(1)}, bf16[256,1024]{1,0:T(8,128)(2,1)S(1)}, u32[]{:S(2)}, u32[]{:S(2)}) collective-permute-start(bf16[256,1024]{1,0:T(8,128)(2,1)S(1)} %bitcast.196), channel_id=1, source_target_pairs={{0,2},{1,3},{2,0},{3,1},{4,6},{5,7},{6,4},{7,5},{8,10},{9,11},{10,... | collective-permute-start | bytes 1572872 | tf_op jit(solution)/shard_map/ppermute | solution.py:78
  56.7 46.2 %collective-permute-start.7 = (bf16[256,1024]{1,0:T(8,128)(2,1)S(1)}, bf16[256,1024]{1,0:T(8,128)(2,1)S(1)}, u32[]{:S(2)}, u32[]{:S(2)}) collective-permute-start(bf16[256,1024]{1,0:T(8,128)(2,1)S(1)} %bitcast.197), channel_id=1, source_target_pairs={{0,3},{1,2},{2,1},{3,0},{4,7},{5,6},{6,5},{7,4},{8,11},{9,10},{10,... | collective-permute-start | bytes 1572872 | tf_op jit(solution)/shard_map/ppermute | solution.py:78
  59.5 45.5 %all-to-all-start.2 = ((bf16[8,64,1024]{2,1,0:T(8,128)(2,1)}), bf16[8,64,1024]{2,1,0:T(8,128)(2,1)}, u32[]{:S(2)}, u32[]{:S(2)}) async-start(bf16[8,64,1024]{2,1,0:T(8,128)(2,1)} %bitcast.201), calls=%async_computation.2 | async-start | bytes 2097152 | tf_op jit(solution)/shard_map/all_to_all | solution.py:129
  105.0 17.3 %all-to-all-start.4 = ((bf16[8,64,1024]{2,1,0:T(8,128)(2,1)}), bf16[8,64,1024]{2,1,0:T(8,128)(2,1)}, u32[]{:S(2)}, u32[]{:S(2)}) async-start(bf16[8,64,1024]{2,1,0:T(8,128)(2,1)} %bitcast.203), calls=%async_computation.4 | async-start | bytes 2097152 | tf_op jit(solution)/shard_map/all_to_all | solution.py:129
  122.3 18.9 %all-to-all-start.6 = ((bf16[8,64,1024]{2,1,0:T(8,128)(2,1)}), bf16[8,64,1024]{2,1,0:T(8,128)(2,1)S(1)}, u32[]{:S(2)}, u32[]{:S(2)}) async-start(bf16[8,64,1024]{2,1,0:T(8,128)(2,1)} %bitcast.202), calls=%async_computation.6 | async-start | bytes 2097152 | tf_op jit(solution)/shard_map/all_to_all | solution.py:129
  141.2 18.9 %all-to-all-start.8 = ((bf16[8,64,1024]{2,1,0:T(8,128)(2,1)}), bf16[8,64,1024]{2,1,0:T(8,128)(2,1)S(1)}, u32[]{:S(2)}, u32[]{:S(2)}) async-start(bf16[8,64,1024]{2,1,0:T(8,128)(2,1)} %bitcast.48), calls=%async_computation.8 | async-start | bytes 2097152 | tf_op jit(solution)/shard_map/all_to_all | solution.py:129
  160.0 1.0 copy-start.4
  161.1 18.9 %all-to-all-start.5 = ((bf16[8,64,1024]{2,1,0:T(8,128)(2,1)}), bf16[8,64,1024]{2,1,0:T(8,128)(2,1)S(1)}, u32[]{:S(2)}, u32[]{:S(2)}) async-start(bf16[8,64,1024]{2,1,0:T(8,128)(2,1)} %bitcast.209), calls=%async_computation.5 | async-start | bytes 2097152 | tf_op jit(solution)/shard_map/all_to_all | solution.py:140
  180.0 1.0 copy-start.3
  180.9 18.9 %all-to-all-start.7 = ((bf16[8,64,1024]{2,1,0:T(8,128)(2,1)}), bf16[8,64,1024]{2,1,0:T(8,128)(2,1)S(1)}, u32[]{:S(2)}, u32[]{:S(2)}) async-start(bf16[8,64,1024]{2,1,0:T(8,128)(2,1)} %bitcast.210), calls=%async_computation.7 | async-start | bytes 2097152 | tf_op jit(solution)/shard_map/all_to_all | solution.py:140
  199.8 18.9 %all-to-all-start.9 = ((bf16[8,64,1024]{2,1,0:T(8,128)(2,1)}), bf16[8,64,1024]{2,1,0:T(8,128)(2,1)S(1)}, u32[]{:S(2)}, u32[]{:S(2)}) async-start(bf16[8,64,1024]{2,1,0:T(8,128)(2,1)} %bitcast.208), calls=%async_computation.9 | async-start | bytes 2097152 | tf_op jit(solution)/shard_map/all_to_all | solution.py:140
  216.7 21.6 %collective-permute-start.2 = (bf16[256,1024]{1,0:T(8,128)(2,1)}, bf16[256,1024]{1,0:T(8,128)(2,1)}, u32[]{:S(2)}, u32[]{:S(2)}) collective-permute-start(bf16[256,1024]{1,0:T(8,128)(2,1)} %fusion.70), channel_id=1, source_target_pairs={{0,1},{1,0},{2,3},{3,2},{4,5},{5,4},{6,7},{7,6},{8,9},{9,8},{10,11... | collective-permute-start | bytes 1572872 | tf_op jit(solution)/shard_map/ppermute | solution.py:78
  218.7 7.0 %copy-start.2 = (bf16[8,64,1024]{2,1,0:T(8,128)(2,1)}, bf16[8,64,1024]{2,1,0:T(8,128)(2,1)S(1)}, u32[]{:S(2)}) copy-start(bf16[8,64,1024]{2,1,0:T(8,128)(2,1)S(1)} %all-to-all-done.9) | copy-start | bytes 3145732
  218.7 19.6 %all-to-all-start.3 = ((bf16[8,64,1024]{2,1,0:T(8,128)(2,1)}), bf16[8,64,1024]{2,1,0:T(8,128)(2,1)}, u32[]{:S(2)}, u32[]{:S(2)}) async-start(bf16[8,64,1024]{2,1,0:T(8,128)(2,1)} %bitcast.206), calls=%async_computation.3 | async-start | bytes 2097152 | tf_op jit(solution)/shard_map/all_to_all | solution.py:140
  225.7 35.1 %collective-permute-start.5 = (bf16[256,1024]{1,0:T(8,128)(2,1)}, bf16[256,1024]{1,0:T(8,128)(2,1)}, u32[]{:S(2)}, u32[]{:S(2)}) collective-permute-start(bf16[256,1024]{1,0:T(8,128)(2,1)} %fusion.71), channel_id=1, source_target_pairs={{0,2},{1,3},{2,0},{3,1},{4,6},{5,7},{6,4},{7,5},{8,10},{9,11},{10,... | collective-permute-start | bytes 1572872 | tf_op jit(solution)/shard_map/ppermute | solution.py:78
  225.7 50.9 %copy-start.1 = (bf16[1024,1024]{1,0:T(8,128)(2,1)S(1)}, bf16[1024,1024]{1,0:T(8,128)(2,1)}, u32[]{:S(2)}) copy-start(bf16[1024,1024]{1,0:T(8,128)(2,1)} %param.11) | copy-start | bytes 6291460
  228.3 45.1 %collective-permute-start.8 = (bf16[256,1024]{1,0:T(8,128)(2,1)}, bf16[256,1024]{1,0:T(8,128)(2,1)}, u32[]{:S(2)}, u32[]{:S(2)}) collective-permute-start(bf16[256,1024]{1,0:T(8,128)(2,1)} %fusion.72), channel_id=1, source_target_pairs={{0,3},{1,2},{2,1},{3,0},{4,7},{5,6},{6,5},{7,4},{8,11},{9,10},{10,... | collective-permute-start | bytes 1572872 | tf_op jit(solution)/shard_map/ppermute | solution.py:78
